TPU v7x, 256 devices: a whole 4x4x8 slice. The times are simulated.
256 devices in a mesh: pairs: 32 (over x, z), tm: 8 (over y, core).
Axes of the slice: x: 4, y: 4, z: 8, core: 2. Of those that a mesh axis runs over, the one named last changes fastest.
Arguments:
- traces: float32 [16, 2048, 6144], P('tm', 'pairs'), may hold values from -64 to 64
- station_slot: int32 [2048], replicated, may hold values from 0 to 2047, as said below
- pair_stations: int32 [2048, 2], P('pairs'), may hold values from 0 to 2047, as said below
Outputs:
- correlation_stack: float32 [2048, 2048], P('tm', 'pairs')
Inputs may be any that keep to these rules, and one draw needn't show every extreme that they name: `station_slot`: A permutation: rows r * 64 to (r + 1) * 64 - 1 of traces are the stations of owner r. `pair_stations`: in each block of 64 pairs (the pairs of one device), at most 8 of the 128 pair ends name stations whose station_slot // 64 is one value, and in every block one value is named by exactly 8 ends. A pair may name one station twice.
All inputs are finite; a program needn't handle non-finite values.
Results may differ from a plain program's by a relative error of at most 0.011.
Values may be sent and summed in bfloat16 or wider, within the bound.
No kernel may reach another device: no remote copies, remote signals or barrier semaphores. Data moves between devices by JAX's collectives and lax.ppermute only.
A program may use at most 64 MiB of HBM per device.

v0:
```python
import math
import jax
import jax.numpy as jnp
from jax import lax
from jax.sharding import PartitionSpec as P

F = 1536
FLO = 32
LAG = 1024
two_pi = 6.283185307179586


def tapered_rows(traces):
    length = traces.shape[-1]
    sample_times = lax.iota(jnp.int32, length).astype(jnp.float32)
    hann_window = 0.5 - 0.5 * jnp.cos((sample_times + 0.5) * (two_pi / length))
    centred = traces - jnp.mean(traces, axis=-1, keepdims=True)
    return (centred * hann_window).astype(jnp.bfloat16)


def forward_table(first_row, row_count, length, first_bin, bins):
    sample_times = first_row + lax.iota(jnp.int32, row_count)
    frequencies = first_bin + lax.iota(jnp.int32, bins)
    phases = sample_times[:, None] * frequencies[None, :] % length
    angles = phases.astype(jnp.float32) * (two_pi / length)
    return jnp.concatenate([jnp.cos(angles), -jnp.sin(angles)], axis=1).astype(jnp.bfloat16)


def whiten(spectrum, bins):
    real_part = spectrum[..., :bins]
    imag_part = spectrum[..., bins:]
    energy = real_part * real_part + imag_part * imag_part
    water_level = jnp.mean(energy, axis=-1, keepdims=True)
    scaling = lax.rsqrt(energy + 0.1 * water_level + 1e-06)
    return jnp.concatenate([real_part * scaling, imag_part * scaling], axis=-1).astype(jnp.bfloat16)


def whiten_spectra(tapered, first_bin, bins):
    length = tapered.shape[1]
    block_rows = min(512, length)

    def add_block(step_index, running):
        first_row = step_index * block_rows
        segment = lax.dynamic_slice_in_dim(tapered, first_row, block_rows, 1)
        cos_table = forward_table(first_row, block_rows, length, first_bin, bins)
        return running + jnp.dot(segment, cos_table, preferred_element_type=jnp.float32)

    spectrum = lax.fori_loop(
        0, length // block_rows, add_block, jnp.zeros((tapered.shape[0], 2 * bins), jnp.float32)
    )
    return whiten(spectrum, bins)


def cross_spectra(left_ends, right_ends, bins):
    left_real = left_ends[..., :bins].astype(jnp.float32)
    left_imag = left_ends[..., bins:].astype(jnp.float32)
    right_real = right_ends[..., :bins].astype(jnp.float32)
    right_imag = right_ends[..., bins:].astype(jnp.float32)
    return jnp.concatenate(
        [
            left_real * right_real + left_imag * right_imag,
            left_imag * right_real - left_real * right_imag,
        ],
        axis=-1,
    )


def lag_block(stacked, first_row, row_count, first_bin, bins, length, half_span):
    lag_values = first_row + lax.iota(jnp.int32, row_count) - half_span
    frequencies = first_bin + lax.iota(jnp.int32, bins)
    phases = lag_values[:, None] * frequencies[None, :] % length
    angles = phases.astype(jnp.float32) * (two_pi / length)
    lag_table = jnp.concatenate([jnp.cos(angles), -jnp.sin(angles)], axis=1)
    return lax.dot_general(
        lag_table,
        stacked,
        (((1,), (1,)), ((), ())),
        precision=lax.Precision.HIGHEST,
        preferred_element_type=jnp.float32,
    )


def lag_rows(stacked, row_count, block_rows, length):

    def one_block(block_index):
        return lag_block(stacked, block_index * block_rows, block_rows, FLO, F, length, LAG)

    pieces = lax.map(one_block, jnp.arange(row_count // block_rows, dtype=jnp.int32))
    return pieces.reshape(row_count, stacked.shape[0])


def on_device(traces, station_slot, pair_stations):
    window_count, station_count, length = traces.shape
    pair_count = pair_stations.shape[0]
    blocks = lax.axis_size("pairs")
    capacity = 4 * pair_count // blocks
    own_index = lax.axis_index("pairs")
    every_pair = lax.all_gather(pair_stations, "pairs", axis=0, tiled=True)
    slot_ids = station_slot[every_pair.reshape(blocks, 2 * pair_count)]
    owners = slot_ids // station_count
    local_rows = slot_ids % station_count
    onehot = (owners[:, :, None] == lax.iota(jnp.int32, blocks)[None, None, :]).astype(jnp.int32)
    end_ranks = jnp.sum((jnp.cumsum(onehot, axis=1) - onehot) * onehot, axis=2)
    wanted = (owners == own_index)[:, :, None] & (
        end_ranks[:, :, None] == lax.iota(jnp.int32, capacity)[None, None, :]
    )
    send_rows = jnp.sum(jnp.where(wanted, local_rows[:, :, None], 0), axis=1)
    own_owners = lax.dynamic_index_in_dim(owners, own_index, 0, keepdims=False)
    own_ranks = lax.dynamic_index_in_dim(end_ranks, own_index, 0, keepdims=False)
    positions = own_owners * capacity + own_ranks
    tapered = tapered_rows(traces).reshape(window_count * station_count, length)
    spectra = whiten_spectra(tapered, FLO, F).reshape(window_count, station_count, 2 * F)
    received = lax.all_to_all(
        spectra[:, send_rows], "pairs", split_axis=1, concat_axis=1, tiled=True
    )
    held_windows = received.shape[0]
    flattened = received.reshape(held_windows, blocks * capacity, 2 * F)
    pair_ends = flattened[:, positions].reshape(held_windows, pair_count, 2, 2 * F)
    cross_terms = cross_spectra(pair_ends[:, :, 0], pair_ends[:, :, 1], F)
    stacked = jnp.sum(cross_terms, axis=0)
    lag_share = 2 * LAG // lax.axis_size("tm")
    normalizer = 1.0 / math.sqrt(F * window_count * lax.axis_size("tm"))
    block_rows = min(256, lag_share)
    return lax.psum_scatter(
        lag_rows(stacked, lax.axis_size("tm") * lag_share, block_rows, length) * normalizer,
        "tm",
        scatter_dimension=0,
        tiled=True,
    )


def solution(mesh):
    in_specs = (P("tm", "pairs", None), P(), P("pairs", None))
    out_specs = P("tm", "pairs")
    return jax.shard_map(
        on_device, mesh=mesh, in_specs=in_specs, out_specs=out_specs, check_vma=False
    )
```

profile of v0, /device:TPU:2, one launch (start us, length us, event | category | flops | bytes accessed | tf_op | source)
XLA Modules:
  0.0 505.4 jit_solution(11358334564074070772)
XLA Ops:
  6.7 2.3 reduce_sum.47
  9.5 1.5 multiply_convert_fusion
  11.0 200.6 %while.29 = (s32[]{:T(128)}, f32[128,3072]{1,0:T(8,128)}, bf16[128,6144]{1,0:T(8,128)(2,1)}, s32[]{:T(128)}, s32[]{:T(128)}, /*index=5*/s32[]{:T(128)}, s32[]{:T(128)}) while((s32[]{:T(128)}, f32[128,3072]{1,0:T(8,128)}, bf16[128,6144]{1,0:T(8,128)(2,1)}, s32[]{:T(128)}, s32[]{:T(128)}, /*index=5*/s32[]{:T(128)}, s32[]{:T(128)}) %tuple.80), condition=%wide.region_2.3_spmd.clone, body=%wide.region_1.2_spmd.clone.sunk | while | flops 419170304 | bytes 9584781 | solution.py:48
  11.0 13.5 %cosine_convert_fusion.2 = (bf16[512,1536]{1,0:T(8,128)(2,1)S(1)}, bf16[512,1536]{1,0:T(8,128)(2,1)S(1)}) fusion(s32[1536]{0:T(1024)S(1)} %iota_add_fusion.7, s32[512]{0:T(512)S(1)} %iota_add_fusion.8), kind=kLoop, calls=%fused_computation.29.clone.1 | loop fusion | flops 9437184 | bytes 3153920 | tf_op jit(solution)/shard_map/convert
  24.6 2.6 convolution_add_fusion.2
  27.2 13.5 %cosine_convert_fusion.2 = (bf16[512,1536]{1,0:T(8,128)(2,1)S(1)}, bf16[512,1536]{1,0:T(8,128)(2,1)S(1)}) fusion(s32[1536]{0:T(1024)S(1)} %iota_add_fusion.7, s32[512]{0:T(512)S(1)} %iota_add_fusion.8), kind=kLoop, calls=%fused_computation.29.clone.1 | loop fusion | flops 9437184 | bytes 3153920 | tf_op jit(solution)/shard_map/convert
  40.8 3.2 convolution_add_fusion.2
  44.0 13.5 %cosine_convert_fusion.2 = (bf16[512,1536]{1,0:T(8,128)(2,1)S(1)}, bf16[512,1536]{1,0:T(8,128)(2,1)S(1)}) fusion(s32[1536]{0:T(1024)S(1)} %iota_add_fusion.7, s32[512]{0:T(512)S(1)} %iota_add_fusion.8), kind=kLoop, calls=%fused_computation.29.clone.1 | loop fusion | flops 9437184 | bytes 3153920 | tf_op jit(solution)/shard_map/convert
  57.5 3.2 convolution_add_fusion.2
  60.8 13.5 %cosine_convert_fusion.2 = (bf16[512,1536]{1,0:T(8,128)(2,1)S(1)}, bf16[512,1536]{1,0:T(8,128)(2,1)S(1)}) fusion(s32[1536]{0:T(1024)S(1)} %iota_add_fusion.7, s32[512]{0:T(512)S(1)} %iota_add_fusion.8), kind=kLoop, calls=%fused_computation.29.clone.1 | loop fusion | flops 9437184 | bytes 3153920 | tf_op jit(solution)/shard_map/convert
  74.3 3.2 convolution_add_fusion.2
  77.5 13.5 %cosine_convert_fusion.2 = (bf16[512,1536]{1,0:T(8,128)(2,1)S(1)}, bf16[512,1536]{1,0:T(8,128)(2,1)S(1)}) fusion(s32[1536]{0:T(1024)S(1)} %iota_add_fusion.7, s32[512]{0:T(512)S(1)} %iota_add_fusion.8), kind=kLoop, calls=%fused_computation.29.clone.1 | loop fusion | flops 9437184 | bytes 3153920 | tf_op jit(solution)/shard_map/convert
  91.1 3.2 convolution_add_fusion.2
  94.3 13.5 %cosine_convert_fusion.2 = (bf16[512,1536]{1,0:T(8,128)(2,1)S(1)}, bf16[512,1536]{1,0:T(8,128)(2,1)S(1)}) fusion(s32[1536]{0:T(1024)S(1)} %iota_add_fusion.7, s32[512]{0:T(512)S(1)} %iota_add_fusion.8), kind=kLoop, calls=%fused_computation.29.clone.1 | loop fusion | flops 9437184 | bytes 3153920 | tf_op jit(solution)/shard_map/convert
  107.8 3.2 convolution_add_fusion.2
  111.1 13.5 %cosine_convert_fusion.2 = (bf16[512,1536]{1,0:T(8,128)(2,1)S(1)}, bf16[512,1536]{1,0:T(8,128)(2,1)S(1)}) fusion(s32[1536]{0:T(1024)S(1)} %iota_add_fusion.7, s32[512]{0:T(512)S(1)} %iota_add_fusion.8), kind=kLoop, calls=%fused_computation.29.clone.1 | loop fusion | flops 9437184 | bytes 3153920 | tf_op jit(solution)/shard_map/convert
  124.6 3.2 convolution_add_fusion.2
  127.8 13.5 %cosine_convert_fusion.2 = (bf16[512,1536]{1,0:T(8,128)(2,1)S(1)}, bf16[512,1536]{1,0:T(8,128)(2,1)S(1)}) fusion(s32[1536]{0:T(1024)S(1)} %iota_add_fusion.7, s32[512]{0:T(512)S(1)} %iota_add_fusion.8), kind=kLoop, calls=%fused_computation.29.clone.1 | loop fusion | flops 9437184 | bytes 3153920 | tf_op jit(solution)/shard_map/convert
  141.4 3.2 convolution_add_fusion.2
  144.6 13.5 %cosine_convert_fusion.2 = (bf16[512,1536]{1,0:T(8,128)(2,1)S(1)}, bf16[512,1536]{1,0:T(8,128)(2,1)S(1)}) fusion(s32[1536]{0:T(1024)S(1)} %iota_add_fusion.7, s32[512]{0:T(512)S(1)} %iota_add_fusion.8), kind=kLoop, calls=%fused_computation.29.clone.1 | loop fusion | flops 9437184 | bytes 3153920 | tf_op jit(solution)/shard_map/convert
  158.1 3.2 convolution_add_fusion.2
  161.4 13.5 %cosine_convert_fusion.2 = (bf16[512,1536]{1,0:T(8,128)(2,1)S(1)}, bf16[512,1536]{1,0:T(8,128)(2,1)S(1)}) fusion(s32[1536]{0:T(1024)S(1)} %iota_add_fusion.7, s32[512]{0:T(512)S(1)} %iota_add_fusion.8), kind=kLoop, calls=%fused_computation.29.clone.1 | loop fusion | flops 9437184 | bytes 3153920 | tf_op jit(solution)/shard_map/convert
  174.9 3.2 convolution_add_fusion.2
  178.1 13.5 %cosine_convert_fusion.2 = (bf16[512,1536]{1,0:T(8,128)(2,1)S(1)}, bf16[512,1536]{1,0:T(8,128)(2,1)S(1)}) fusion(s32[1536]{0:T(1024)S(1)} %iota_add_fusion.7, s32[512]{0:T(512)S(1)} %iota_add_fusion.8), kind=kLoop, calls=%fused_computation.29.clone.1 | loop fusion | flops 9437184 | bytes 3153920 | tf_op jit(solution)/shard_map/convert
  191.7 3.2 convolution_add_fusion.2
  194.9 13.5 %cosine_convert_fusion.2 = (bf16[512,1536]{1,0:T(8,128)(2,1)S(1)}, bf16[512,1536]{1,0:T(8,128)(2,1)S(1)}) fusion(s32[1536]{0:T(1024)S(1)} %iota_add_fusion.7, s32[512]{0:T(512)S(1)} %iota_add_fusion.8), kind=kLoop, calls=%fused_computation.29.clone.1 | loop fusion | flops 9437184 | bytes 3153920 | tf_op jit(solution)/shard_map/convert
  208.4 3.2 convolution_add_fusion.2
  211.7 1.7 fusion.40
  214.7 45.7 %all-gather = s32[32,64,2]{1,2,0:T(2,128)S(1)} all-gather(s32[1,64,2]{1,2,0:T(2,128)S(1)} %bitcast.77), channel_id=1, replica_groups=mesh['pairs'=32,'tm'=8] {'pairs'}, dimensions={0}, use_global_device_ids=true | all-gather | bytes 16896 | tf_op jit(solution)/shard_map/all_gather | solution.py:98
  260.6 23.0 %gather_fusion = s32[4096]{0:T(1024)S(1)} fusion(s32[2048]{0:T(1024)S(1)} %copy-done, s32[4096]{0:T(1024)S(1)} %bitcast_clamp_fusion), kind=kCustom, calls=%fused_computation | custom fusion | bytes 49152 | tf_op jit(solution)/shard_map/gather | solution.py:99
  283.7 3.3 fusion.31
  287.9 0.7 pad_maximum_fusion
  288.6 12.9 %gather_fusion.1 = bf16[256,2,3072]{2,1,0:T(2,128)(2,1)} fusion(bf16[2,64,3072]{2,0,1:T(2,128)(2,1)S(1)} %pad_maximum_fusion, s32[1024]{0:T(1024)S(1)} %pad_clamp_fusion.1), kind=kCustom, calls=%fused_computation.1 | custom fusion | bytes 6292480 | tf_op jit(solution)/shard_map/gather | solution.py:114
  301.4 6.9 %all-to-all-start = ((bf16[2,32,8,3072]{3,0,2,1:T(2,128)(2,1)}), bf16[2,32,8,3072]{3,0,2,1:T(2,128)(2,1)S(1)}, u32[]{:S(2)}, u32[]{:S(2)}) async-start(bf16[2,32,8,3072]{3,0,2,1:T(2,128)(2,1)} %bitcast.69), calls=%async_computation | async-start | bytes 6291456 | tf_op jit(solution)/shard_map/all_to_all | solution.py:113
  308.7 62.0 %all-to-all-done = bf16[2,32,8,3072]{3,0,2,1:T(2,128)(2,1)S(1)} async-done(((bf16[2,32,8,3072]{3,0,2,1:T(2,128)(2,1)}), bf16[2,32,8,3072]{3,0,2,1:T(2,128)(2,1)S(1)}, u32[]{:S(2)}, u32[]{:S(2)}) %all-to-all-start) | async-done | bytes 3145760 | tf_op jit(solution)/shard_map/all_to_all | solution.py:113
  370.6 4.8 gather_fusion.2
  375.4 2.4 fusion.41
  378.6 0.9 copy-done.3
  379.5 86.6 %while.28 = (s32[]{:T(128)}, f32[8,256,64]{1,2,0:T(8,128)S(1)}, s32[8]{0:T(128)S(1)}, f32[64,3072]{1,0:T(8,128)S(1)}, s32[]{:T(128)}, /*index=5*/s32[1]{0:T(128)}) while((s32[]{:T(128)}, f32[8,256,64]{1,2,0:T(8,128)S(1)}, s32[8]{0:T(128)S(1)}, f32[64,3072]{1,0:T(8,128)S(1)}, s32[]{:T(128)}, /*index=5*/s32[1]{0:T(128)}) %tuple.81), condition=%wide.region_9.10_spmd, body=%wide.region_8.9_spmd.sunk | while | flops 608700416 | bytes 7157861 | solution.py:88
  380.9 6.4 %fusion.51 = (f32[256,1536]{1,0:T(8,128)S(1)}, f32[256,1536]{1,0:T(8,128)S(1)}) fusion(s32[1536]{0:T(1024)S(1)} %iota_add_fusion.6, s32[256]{0:T(256)S(1)} %add_add_fusion.2), kind=kLoop, calls=%fused_computation.14.clone.1 | loop fusion | flops 3932160 | bytes 3152896 | tf_op jit(solution)/shard_map/while/body/eval_jaxpr/cos | solution.py:73
  387.3 3.0 fusion.52
  390.3 0.7 dynamic_slice.33
  391.7 6.4 %fusion.51 = (f32[256,1536]{1,0:T(8,128)S(1)}, f32[256,1536]{1,0:T(8,128)S(1)}) fusion(s32[1536]{0:T(1024)S(1)} %iota_add_fusion.6, s32[256]{0:T(256)S(1)} %add_add_fusion.2), kind=kLoop, calls=%fused_computation.14.clone.1 | loop fusion | flops 3932160 | bytes 3152896 | tf_op jit(solution)/shard_map/while/body/eval_jaxpr/cos | solution.py:73
  398.1 3.0 fusion.52
  401.2 0.7 dynamic_slice.33
  402.5 6.4 %fusion.51 = (f32[256,1536]{1,0:T(8,128)S(1)}, f32[256,1536]{1,0:T(8,128)S(1)}) fusion(s32[1536]{0:T(1024)S(1)} %iota_add_fusion.6, s32[256]{0:T(256)S(1)} %add_add_fusion.2), kind=kLoop, calls=%fused_computation.14.clone.1 | loop fusion | flops 3932160 | bytes 3152896 | tf_op jit(solution)/shard_map/while/body/eval_jaxpr/cos | solution.py:73
  409.0 3.0 fusion.52
  412.0 0.7 dynamic_slice.33
  413.4 6.4 %fusion.51 = (f32[256,1536]{1,0:T(8,128)S(1)}, f32[256,1536]{1,0:T(8,128)S(1)}) fusion(s32[1536]{0:T(1024)S(1)} %iota_add_fusion.6, s32[256]{0:T(256)S(1)} %add_add_fusion.2), kind=kLoop, calls=%fused_computation.14.clone.1 | loop fusion | flops 3932160 | bytes 3152896 | tf_op jit(solution)/shard_map/while/body/eval_jaxpr/cos | solution.py:73
  419.8 3.0 fusion.52
  422.8 0.7 dynamic_slice.33
  424.2 6.4 %fusion.51 = (f32[256,1536]{1,0:T(8,128)S(1)}, f32[256,1536]{1,0:T(8,128)S(1)}) fusion(s32[1536]{0:T(1024)S(1)} %iota_add_fusion.6, s32[256]{0:T(256)S(1)} %add_add_fusion.2), kind=kLoop, calls=%fused_computation.14.clone.1 | loop fusion | flops 3932160 | bytes 3152896 | tf_op jit(solution)/shard_map/while/body/eval_jaxpr/cos | solution.py:73
  430.6 3.0 fusion.52
  433.6 0.7 dynamic_slice.33
  435.0 6.4 %fusion.51 = (f32[256,1536]{1,0:T(8,128)S(1)}, f32[256,1536]{1,0:T(8,128)S(1)}) fusion(s32[1536]{0:T(1024)S(1)} %iota_add_fusion.6, s32[256]{0:T(256)S(1)} %add_add_fusion.2), kind=kLoop, calls=%fused_computation.14.clone.1 | loop fusion | flops 3932160 | bytes 3152896 | tf_op jit(solution)/shard_map/while/body/eval_jaxpr/cos | solution.py:73
  441.4 3.0 fusion.52
  444.4 0.7 dynamic_slice.33
  445.8 6.4 %fusion.51 = (f32[256,1536]{1,0:T(8,128)S(1)}, f32[256,1536]{1,0:T(8,128)S(1)}) fusion(s32[1536]{0:T(1024)S(1)} %iota_add_fusion.6, s32[256]{0:T(256)S(1)} %add_add_fusion.2), kind=kLoop, calls=%fused_computation.14.clone.1 | loop fusion | flops 3932160 | bytes 3152896 | tf_op jit(solution)/shard_map/while/body/eval_jaxpr/cos | solution.py:73
  452.3 3.0 fusion.52
  455.3 0.7 dynamic_slice.33
  456.6 6.4 %fusion.51 = (f32[256,1536]{1,0:T(8,128)S(1)}, f32[256,1536]{1,0:T(8,128)S(1)}) fusion(s32[1536]{0:T(1024)S(1)} %iota_add_fusion.6, s32[256]{0:T(256)S(1)} %add_add_fusion.2), kind=kLoop, calls=%fused_computation.14.clone.1 | loop fusion | flops 3932160 | bytes 3152896 | tf_op jit(solution)/shard_map/while/body/eval_jaxpr/cos | solution.py:73
  463.1 3.0 fusion.52
  466.1 0.8 copy.71
  467.0 31.6 %reduce-scatter.2.cloned.1.call-done = f32[256,64]{0,1:T(8,128)} async-done(((f32[2048,64]{0,1:T(8,128)}), f32[256,64]{0,1:T(8,128)}) %reduce-scatter.2.cloned.1.call-update) | async-done | bytes 65552 | tf_op jit(solution)/shard_map/reduce_scatter | solution.py:124
  (79 shorter events, 4.9 us)
Async XLA Ops:
  6.5 254.0 %copy-start = (s32[2048]{0:T(1024)S(1)}, s32[2048]{0:T(1024)}, u32[]{:S(2)}) copy-start(s32[2048]{0:T(1024)} %param.8) | copy-start | bytes 24580
  6.7 2.8 copy-start.1
  211.7 1.9 copy-start.2
  213.5 1.1 copy-start.4
  301.4 69.2 %all-to-all-start = ((bf16[2,32,8,3072]{3,0,2,1:T(2,128)(2,1)}), bf16[2,32,8,3072]{3,0,2,1:T(2,128)(2,1)S(1)}, u32[]{:S(2)}, u32[]{:S(2)}) async-start(bf16[2,32,8,3072]{3,0,2,1:T(2,128)(2,1)} %bitcast.69), calls=%async_computation | async-start | bytes 6291456 | tf_op jit(solution)/shard_map/all_to_all | solution.py:113
  308.4 190.2 %reduce-scatter.2.cloned.1.call-start = ((), (), s32[]{:S(2)}) async-start(), calls=%async_computation.2 | async-start | bytes 589824 | tf_op jit(solution)/shard_map/reduce_scatter | solution.py:124
  378.5 1.0 copy-start.3
Sparse Core Ops, SparseCore 0:
  467.1 31.3 reduce-scatter.1
where the time goes:
time: 506 us; the launch traced here: 505 us
  other arithmetic  225 us (44%)
  waiting for transfers between devices  93.5 us (18%)
  matrix products  62.1 us (12%)
  local copies, waits for them, and re-layouts  52.5 us (10%)
  blocking collectives  45.7 us (9%)
  between operations  13.6 us (3%)
  starting transfers between devices  7.16 us (1%)
  loops' own time  5.98 us (1%)
    another operation x13, other arithmetic  163 us
    all_to_all x1, waiting for transfers between devices, on_device(): lax.all_to_all(spectra[:, send_rows], 'pairs', split_axis=1, concat_axis=...  62 us
    cos x8, other arithmetic, lag_block(): lag_table = jnp.concatenate([jnp.cos(angles), -jnp.sin(angles)], axis=1)  51.4 us
    all_gather x1, blocking collectives, on_device(): every_pair = lax.all_gather(pair_stations, 'pairs', axis=0, tiled=True)  45.7 us
    dot_general x12, matrix products, add_block(): jnp.dot(segment, cos_table, preferred_element_type=jnp.float32)  38.1 us
    reduce_scatter x1, waiting for transfers between devices, on_device(): lax.psum_scatter(lag_rows(stacked, lax.axis_size('tm') * lag_share, block...  31.6 us
    dot_general x8, matrix products, lag_block(): lax.dot_general(lag_table, stacked, (((1,), (1,)), ((), ())), precision=l...  23.9 us
    gather x1, local copies, waits for them, and re-layouts, on_device(): slot_ids = station_slot[every_pair.reshape(blocks, 2 * pair_count)]  23 us
  transfers between devices with their start and end apart: 2, of which 2 were waited for; matrix products, arithmetic and copies ran while one was open for 0% of the time, Pallas kernels for 0%

commit v1 on v0

--- a/solution.py
+++ b/solution.py
@@ -95,7 +95,9 @@
     blocks = lax.axis_size("pairs")
     capacity = 4 * pair_count // blocks
     own_index = lax.axis_index("pairs")
-    every_pair = lax.all_gather(pair_stations, "pairs", axis=0, tiled=True)
+    every_pair = jnp.concatenate(
+        lax.all_to_all(jnp.stack([pair_stations] * lax.axis_size("pairs")), "pairs", 0, 0), axis=0
+    )
     slot_ids = station_slot[every_pair.reshape(blocks, 2 * pair_count)]
     owners = slot_ids // station_count
     local_rows = slot_ids % station_count

time: 506 us -> 487 us (0.962)
  blocking collectives: 45.7 us -> 0 us
  starting transfers between devices: 7.16 us -> 21.4 us
  waiting for transfers between devices: 93.5 us -> 104 us
    all_gather x1 -> x0, blocking collectives: 45.7 us -> none  [on_device(): every_pair = lax.all_gather(pair_stations, 'pairs', axis=0, tiled=True)]
    all_to_all x0 -> x1, starting transfers between devices: none -> 11.6 us  [on_device(): lax.all_to_all(jnp.stack([pair_stations] * lax.axis_size('pairs')), 'pair...]
    all_to_all x1, waiting for transfers between devices: 62 us -> 71.6 us  [on_device(): lax.all_to_all(spectra[:, send_rows], 'pairs', split_axis=1, concat_axis=...]
  transfers between devices with their start and end apart: 2 -> 3, of which waited for: 2 -> 2; matrix products, arithmetic and copies ran while one was open for 0% -> 43% of each run, Pallas kernels for 0% -> 0%
where the time goes in v1:
time: 487 us; the launch traced here: 486 us
  other arithmetic  226 us (46%)
  waiting for transfers between devices  104 us (21%)
  matrix products  62 us (13%)
  local copies, waits for them, and re-layouts  54 us (11%)
  starting transfers between devices  21.4 us (4%)
  between operations  13.6 us (3%)
  loops' own time  5.63 us (1%)
    another operation x13, other arithmetic  163 us
    all_to_all x1, waiting for transfers between devices, on_device(): lax.all_to_all(spectra[:, send_rows], 'pairs', split_axis=1, concat_axis=...  71.6 us
    cos x8, other arithmetic, lag_block(): lag_table = jnp.concatenate([jnp.cos(angles), -jnp.sin(angles)], axis=1)  51.4 us
    dot_general x12, matrix products, add_block(): jnp.dot(segment, cos_table, preferred_element_type=jnp.float32)  38.1 us
    reduce_scatter x1, waiting for transfers between devices, on_device(): lax.psum_scatter(lag_rows(stacked, lax.axis_size('tm') * lag_share, block...  32.4 us
    dot_general x8, matrix products, lag_block(): lax.dot_general(lag_table, stacked, (((1,), (1,)), ((), ())), precision=l...  23.9 us
    gather x1, local copies, waits for them, and re-layouts, on_device(): slot_ids = station_slot[every_pair.reshape(blocks, 2 * pair_count)]  23 us
    gather x1, local copies, waits for them, and re-layouts, on_device(): spectra[:, send_rows]  13 us
  transfers between devices with their start and end apart: 3, of which 2 were waited for; matrix products, arithmetic and copies ran while one was open for 43% of the time, Pallas kernels for 0%

profile of v1, /device:TPU:2, one launch (start us, length us, event | category | flops | bytes accessed | tf_op | source)
XLA Modules:
  0.0 486.4 jit_solution(18329330085008356647)
XLA Ops:
  6.5 0.7 broadcast_bitcast_fusion
  7.2 0.7 reshape.191
  7.9 11.6 %all-to-all-start = ((s32[32,1,128]{2,1,0:T(1,128)}), s32[32,1,128]{2,1,0:T(1,128)S(1)}, u32[]{:S(2)}, u32[]{:S(2)}) async-start(s32[32,1,128]{2,1,0:T(1,128)} %reshape.191), calls=%async_computation | async-start | bytes 32768 | tf_op jit(solution)/shard_map/all_to_all | solution.py:99
  19.7 2.3 reduce_sum.47
  22.5 1.5 multiply_convert_fusion
  24.1 200.6 %while.29 = (s32[]{:T(128)}, f32[128,3072]{1,0:T(8,128)}, bf16[128,6144]{1,0:T(8,128)(2,1)}, s32[]{:T(128)}, s32[]{:T(128)}, /*index=5*/s32[]{:T(128)}, s32[]{:T(128)}) while((s32[]{:T(128)}, f32[128,3072]{1,0:T(8,128)}, bf16[128,6144]{1,0:T(8,128)(2,1)}, s32[]{:T(128)}, s32[]{:T(128)}, /*index=5*/s32[]{:T(128)}, s32[]{:T(128)}) %tuple.80), condition=%wide.region_2.3_spmd.clone, body=%wide.region_1.2_spmd.clone.sunk | while | flops 419170304 | bytes 9584781 | solution.py:48
  24.1 13.5 %cosine_convert_fusion.2 = (bf16[512,1536]{1,0:T(8,128)(2,1)S(1)}, bf16[512,1536]{1,0:T(8,128)(2,1)S(1)}) fusion(s32[1536]{0:T(1024)S(1)} %iota_add_fusion.7, s32[512]{0:T(512)S(1)} %iota_add_fusion.8), kind=kLoop, calls=%fused_computation.29.clone.1 | loop fusion | flops 9437184 | bytes 3153920 | tf_op jit(solution)/shard_map/convert
  37.6 2.6 convolution_add_fusion.2
  40.3 13.5 %cosine_convert_fusion.2 = (bf16[512,1536]{1,0:T(8,128)(2,1)S(1)}, bf16[512,1536]{1,0:T(8,128)(2,1)S(1)}) fusion(s32[1536]{0:T(1024)S(1)} %iota_add_fusion.7, s32[512]{0:T(512)S(1)} %iota_add_fusion.8), kind=kLoop, calls=%fused_computation.29.clone.1 | loop fusion | flops 9437184 | bytes 3153920 | tf_op jit(solution)/shard_map/convert
  53.8 3.2 convolution_add_fusion.2
  57.0 13.5 %cosine_convert_fusion.2 = (bf16[512,1536]{1,0:T(8,128)(2,1)S(1)}, bf16[512,1536]{1,0:T(8,128)(2,1)S(1)}) fusion(s32[1536]{0:T(1024)S(1)} %iota_add_fusion.7, s32[512]{0:T(512)S(1)} %iota_add_fusion.8), kind=kLoop, calls=%fused_computation.29.clone.1 | loop fusion | flops 9437184 | bytes 3153920 | tf_op jit(solution)/shard_map/convert
  70.6 3.2 convolution_add_fusion.2
  73.8 13.5 %cosine_convert_fusion.2 = (bf16[512,1536]{1,0:T(8,128)(2,1)S(1)}, bf16[512,1536]{1,0:T(8,128)(2,1)S(1)}) fusion(s32[1536]{0:T(1024)S(1)} %iota_add_fusion.7, s32[512]{0:T(512)S(1)} %iota_add_fusion.8), kind=kLoop, calls=%fused_computation.29.clone.1 | loop fusion | flops 9437184 | bytes 3153920 | tf_op jit(solution)/shard_map/convert
  87.3 3.2 convolution_add_fusion.2
  90.6 13.5 %cosine_convert_fusion.2 = (bf16[512,1536]{1,0:T(8,128)(2,1)S(1)}, bf16[512,1536]{1,0:T(8,128)(2,1)S(1)}) fusion(s32[1536]{0:T(1024)S(1)} %iota_add_fusion.7, s32[512]{0:T(512)S(1)} %iota_add_fusion.8), kind=kLoop, calls=%fused_computation.29.clone.1 | loop fusion | flops 9437184 | bytes 3153920 | tf_op jit(solution)/shard_map/convert
  104.1 3.2 convolution_add_fusion.2
  107.3 13.5 %cosine_convert_fusion.2 = (bf16[512,1536]{1,0:T(8,128)(2,1)S(1)}, bf16[512,1536]{1,0:T(8,128)(2,1)S(1)}) fusion(s32[1536]{0:T(1024)S(1)} %iota_add_fusion.7, s32[512]{0:T(512)S(1)} %iota_add_fusion.8), kind=kLoop, calls=%fused_computation.29.clone.1 | loop fusion | flops 9437184 | bytes 3153920 | tf_op jit(solution)/shard_map/convert
  120.9 3.2 convolution_add_fusion.2
  124.1 13.5 %cosine_convert_fusion.2 = (bf16[512,1536]{1,0:T(8,128)(2,1)S(1)}, bf16[512,1536]{1,0:T(8,128)(2,1)S(1)}) fusion(s32[1536]{0:T(1024)S(1)} %iota_add_fusion.7, s32[512]{0:T(512)S(1)} %iota_add_fusion.8), kind=kLoop, calls=%fused_computation.29.clone.1 | loop fusion | flops 9437184 | bytes 3153920 | tf_op jit(solution)/shard_map/convert
  137.6 3.2 convolution_add_fusion.2
  140.9 13.5 %cosine_convert_fusion.2 = (bf16[512,1536]{1,0:T(8,128)(2,1)S(1)}, bf16[512,1536]{1,0:T(8,128)(2,1)S(1)}) fusion(s32[1536]{0:T(1024)S(1)} %iota_add_fusion.7, s32[512]{0:T(512)S(1)} %iota_add_fusion.8), kind=kLoop, calls=%fused_computation.29.clone.1 | loop fusion | flops 9437184 | bytes 3153920 | tf_op jit(solution)/shard_map/convert
  154.4 3.2 convolution_add_fusion.2
  157.6 13.5 %cosine_convert_fusion.2 = (bf16[512,1536]{1,0:T(8,128)(2,1)S(1)}, bf16[512,1536]{1,0:T(8,128)(2,1)S(1)}) fusion(s32[1536]{0:T(1024)S(1)} %iota_add_fusion.7, s32[512]{0:T(512)S(1)} %iota_add_fusion.8), kind=kLoop, calls=%fused_computation.29.clone.1 | loop fusion | flops 9437184 | bytes 3153920 | tf_op jit(solution)/shard_map/convert
  171.2 3.2 convolution_add_fusion.2
  174.4 13.5 %cosine_convert_fusion.2 = (bf16[512,1536]{1,0:T(8,128)(2,1)S(1)}, bf16[512,1536]{1,0:T(8,128)(2,1)S(1)}) fusion(s32[1536]{0:T(1024)S(1)} %iota_add_fusion.7, s32[512]{0:T(512)S(1)} %iota_add_fusion.8), kind=kLoop, calls=%fused_computation.29.clone.1 | loop fusion | flops 9437184 | bytes 3153920 | tf_op jit(solution)/shard_map/convert
  187.9 3.2 convolution_add_fusion.2
  191.2 13.5 %cosine_convert_fusion.2 = (bf16[512,1536]{1,0:T(8,128)(2,1)S(1)}, bf16[512,1536]{1,0:T(8,128)(2,1)S(1)}) fusion(s32[1536]{0:T(1024)S(1)} %iota_add_fusion.7, s32[512]{0:T(512)S(1)} %iota_add_fusion.8), kind=kLoop, calls=%fused_computation.29.clone.1 | loop fusion | flops 9437184 | bytes 3153920 | tf_op jit(solution)/shard_map/convert
  204.7 3.2 convolution_add_fusion.2
  207.9 13.5 %cosine_convert_fusion.2 = (bf16[512,1536]{1,0:T(8,128)(2,1)S(1)}, bf16[512,1536]{1,0:T(8,128)(2,1)S(1)}) fusion(s32[1536]{0:T(1024)S(1)} %iota_add_fusion.7, s32[512]{0:T(512)S(1)} %iota_add_fusion.8), kind=kLoop, calls=%fused_computation.29.clone.1 | loop fusion | flops 9437184 | bytes 3153920 | tf_op jit(solution)/shard_map/convert
  221.5 3.2 convolution_add_fusion.2
  224.7 1.7 fusion.40
  227.7 0.7 pad_maximum_fusion
  228.9 0.7 reduce
  229.9 23.0 %gather_fusion = s32[4096]{0:T(1024)S(1)} fusion(s32[2048]{0:T(1024)S(1)} %copy-done, s32[4096]{0:T(1024)S(1)} %bitcast_clamp_fusion), kind=kCustom, calls=%fused_computation | custom fusion | bytes 49152 | tf_op jit(solution)/shard_map/gather | solution.py:101
  253.1 3.3 fusion.31
  256.5 0.6 select_reduce_fusion
  257.2 13.0 %gather_fusion.1 = bf16[256,2,3072]{2,1,0:T(2,128)(2,1)} fusion(bf16[2,64,3072]{2,0,1:T(2,128)(2,1)S(1)} %pad_maximum_fusion, s32[1024]{0:T(1024)S(1)} %pad_clamp_fusion.1), kind=kCustom, calls=%fused_computation.1 | custom fusion | bytes 6292480 | tf_op jit(solution)/shard_map/gather | solution.py:116
  270.3 9.8 %all-to-all-start.1 = ((bf16[2,32,8,3072]{3,0,2,1:T(2,128)(2,1)}), bf16[2,32,8,3072]{3,0,2,1:T(2,128)(2,1)S(1)}, u32[]{:S(2)}, u32[]{:S(2)}) async-start(bf16[2,32,8,3072]{3,0,2,1:T(2,128)(2,1)} %bitcast.71), calls=%async_computation.1 | async-start | bytes 6291456 | tf_op jit(solution)/shard_map/all_to_all | solution.py:115
  280.1 71.6 %all-to-all-done.1 = bf16[2,32,8,3072]{3,0,2,1:T(2,128)(2,1)S(1)} async-done(((bf16[2,32,8,3072]{3,0,2,1:T(2,128)(2,1)}), bf16[2,32,8,3072]{3,0,2,1:T(2,128)(2,1)S(1)}, u32[]{:S(2)}, u32[]{:S(2)}) %all-to-all-start.1) | async-done | bytes 3145760 | tf_op jit(solution)/shard_map/all_to_all | solution.py:115
  351.7 4.8 gather_fusion.2
  356.5 2.4 fusion.41
  359.7 0.9 copy-done.3
  360.6 85.5 %while.28 = (s32[]{:T(128)}, f32[8,256,64]{1,2,0:T(8,128)S(1)}, s32[8]{0:T(128)S(1)}, f32[64,3072]{1,0:T(8,128)S(1)}, s32[]{:T(128)}, /*index=5*/s32[1]{0:T(128)}) while((s32[]{:T(128)}, f32[8,256,64]{1,2,0:T(8,128)S(1)}, s32[8]{0:T(128)S(1)}, f32[64,3072]{1,0:T(8,128)S(1)}, s32[]{:T(128)}, /*index=5*/s32[1]{0:T(128)}) %tuple.81), condition=%wide.region_9.10_spmd, body=%wide.region_8.9_spmd.sunk | while | flops 608700416 | bytes 7157861 | solution.py:88
  361.9 6.4 %fusion.51 = (f32[256,1536]{1,0:T(8,128)S(1)}, f32[256,1536]{1,0:T(8,128)S(1)}) fusion(s32[1536]{0:T(1024)S(1)} %iota_add_fusion.6, s32[256]{0:T(256)S(1)} %add_add_fusion.2), kind=kLoop, calls=%fused_computation.14.clone.1 | loop fusion | flops 3932160 | bytes 3152896 | tf_op jit(solution)/shard_map/while/body/eval_jaxpr/cos | solution.py:73
  368.3 3.0 fusion.52
  371.3 0.6 dynamic_slice.33
  372.6 6.4 %fusion.51 = (f32[256,1536]{1,0:T(8,128)S(1)}, f32[256,1536]{1,0:T(8,128)S(1)}) fusion(s32[1536]{0:T(1024)S(1)} %iota_add_fusion.6, s32[256]{0:T(256)S(1)} %add_add_fusion.2), kind=kLoop, calls=%fused_computation.14.clone.1 | loop fusion | flops 3932160 | bytes 3152896 | tf_op jit(solution)/shard_map/while/body/eval_jaxpr/cos | solution.py:73
  379.0 3.0 fusion.52
  383.3 6.4 %fusion.51 = (f32[256,1536]{1,0:T(8,128)S(1)}, f32[256,1536]{1,0:T(8,128)S(1)}) fusion(s32[1536]{0:T(1024)S(1)} %iota_add_fusion.6, s32[256]{0:T(256)S(1)} %add_add_fusion.2), kind=kLoop, calls=%fused_computation.14.clone.1 | loop fusion | flops 3932160 | bytes 3152896 | tf_op jit(solution)/shard_map/while/body/eval_jaxpr/cos | solution.py:73
  389.7 3.0 fusion.52
  394.0 6.4 %fusion.51 = (f32[256,1536]{1,0:T(8,128)S(1)}, f32[256,1536]{1,0:T(8,128)S(1)}) fusion(s32[1536]{0:T(1024)S(1)} %iota_add_fusion.6, s32[256]{0:T(256)S(1)} %add_add_fusion.2), kind=kLoop, calls=%fused_computation.14.clone.1 | loop fusion | flops 3932160 | bytes 3152896 | tf_op jit(solution)/shard_map/while/body/eval_jaxpr/cos | solution.py:73
  400.4 3.0 fusion.52
  403.4 0.6 dynamic_slice.33
  404.7 6.4 %fusion.51 = (f32[256,1536]{1,0:T(8,128)S(1)}, f32[256,1536]{1,0:T(8,128)S(1)}) fusion(s32[1536]{0:T(1024)S(1)} %iota_add_fusion.6, s32[256]{0:T(256)S(1)} %add_add_fusion.2), kind=kLoop, calls=%fused_computation.14.clone.1 | loop fusion | flops 3932160 | bytes 3152896 | tf_op jit(solution)/shard_map/while/body/eval_jaxpr/cos | solution.py:73
  411.1 3.0 fusion.52
  414.1 0.6 dynamic_slice.33
  415.4 6.4 %fusion.51 = (f32[256,1536]{1,0:T(8,128)S(1)}, f32[256,1536]{1,0:T(8,128)S(1)}) fusion(s32[1536]{0:T(1024)S(1)} %iota_add_fusion.6, s32[256]{0:T(256)S(1)} %add_add_fusion.2), kind=kLoop, calls=%fused_computation.14.clone.1 | loop fusion | flops 3932160 | bytes 3152896 | tf_op jit(solution)/shard_map/while/body/eval_jaxpr/cos | solution.py:73
  421.8 3.0 fusion.52
  426.1 6.4 %fusion.51 = (f32[256,1536]{1,0:T(8,128)S(1)}, f32[256,1536]{1,0:T(8,128)S(1)}) fusion(s32[1536]{0:T(1024)S(1)} %iota_add_fusion.6, s32[256]{0:T(256)S(1)} %add_add_fusion.2), kind=kLoop, calls=%fused_computation.14.clone.1 | loop fusion | flops 3932160 | bytes 3152896 | tf_op jit(solution)/shard_map/while/body/eval_jaxpr/cos | solution.py:73
  432.5 3.0 fusion.52
  436.8 6.4 %fusion.51 = (f32[256,1536]{1,0:T(8,128)S(1)}, f32[256,1536]{1,0:T(8,128)S(1)}) fusion(s32[1536]{0:T(1024)S(1)} %iota_add_fusion.6, s32[256]{0:T(256)S(1)} %add_add_fusion.2), kind=kLoop, calls=%fused_computation.14.clone.1 | loop fusion | flops 3932160 | bytes 3152896 | tf_op jit(solution)/shard_map/while/body/eval_jaxpr/cos | solution.py:73
  443.2 3.0 fusion.52
  446.2 0.8 copy.71
  447.1 32.4 %reduce-scatter.2.cloned.1.call-done = f32[256,64]{0,1:T(8,128)} async-done(((f32[2048,64]{0,1:T(8,128)}), f32[256,64]{0,1:T(8,128)}) %reduce-scatter.2.cloned.1.call-update) | async-done | bytes 65552 | tf_op jit(solution)/shard_map/reduce_scatter | solution.py:126
  (83 shorter events, 7.0 us)
Async XLA Ops:
  6.5 223.3 %copy-start = (s32[2048]{0:T(1024)S(1)}, s32[2048]{0:T(1024)}, u32[]{:S(2)}) copy-start(s32[2048]{0:T(1024)} %param.8) | copy-start | bytes 24580
  7.9 220.4 %all-to-all-start = ((s32[32,1,128]{2,1,0:T(1,128)}), s32[32,1,128]{2,1,0:T(1,128)S(1)}, u32[]{:S(2)}, u32[]{:S(2)}) async-start(s32[32,1,128]{2,1,0:T(1,128)} %reshape.191), calls=%async_computation | async-start | bytes 32768 | tf_op jit(solution)/shard_map/all_to_all | solution.py:99
  19.7 2.8 copy-start.1
  224.7 1.9 copy-start.2
  270.3 81.5 %all-to-all-start.1 = ((bf16[2,32,8,3072]{3,0,2,1:T(2,128)(2,1)}), bf16[2,32,8,3072]{3,0,2,1:T(2,128)(2,1)S(1)}, u32[]{:S(2)}, u32[]{:S(2)}) async-start(bf16[2,32,8,3072]{3,0,2,1:T(2,128)(2,1)} %bitcast.71), calls=%async_computation.1 | async-start | bytes 6291456 | tf_op jit(solution)/shard_map/all_to_all | solution.py:115
  280.1 199.5 %reduce-scatter.2.cloned.1.call-start = ((), (), s32[]{:S(2)}) async-start(), calls=%async_computation.3 | async-start | bytes 589824 | tf_op jit(solution)/shard_map/reduce_scatter | solution.py:126
  359.6 1.0 copy-start.3
Sparse Core Ops, SparseCore 0:
  447.2 32.2 reduce-scatter.1
